TPU v7x, 256 devices: a whole 4x4x8 slice. The times are simulated.
256 devices in a mesh: dp: 32 (over y, x, core), tensor: 8 (over z).
Axes of the slice: x: 4, y: 4, z: 8, core: 2. Of those that a mesh axis runs over, the one named last changes fastest.
Arguments:
- rank_query: bfloat16 [256, 32, 5120], P('dp', None, 'tensor'), may hold values from -4.5 to 4.5
- rank_key: bfloat16 [256, 32, 5120], P('dp', None, 'tensor'), may hold values from -4.5 to 4.5
- rank_value: bfloat16 [256, 32, 5120], P('dp', None, 'tensor'), may hold values from -6 to 6
- rank_resid: bfloat16 [256, 32, 5120], P(('dp', 'tensor')), may hold values from -4 to 4
- out_weight: bfloat16 [5120, 5120], P('tensor', 'dp'), may hold values from -0.25 to 0.25
- rank_gain: bfloat16 [5120], replicated, may hold values from 0.099609375 to 1.8984375
- score_weight: bfloat16 [5120], replicated, may hold values from -0.078125 to 0.078125
- pair_index: int32 [256, 3], P(('dp', 'tensor')), may hold values from 0 to 31, as said below
- cand_rank: int32 [1024, 8], P('dp'), may hold values from 0 to 7, each once within a row
- cand_len: int32 [1024, 8], P('dp'), may hold values from 1 to 8, 39 in all within a row
- blend_owner: int32 [32, 32], P('dp'), may hold values from 0 to 31, each once within a row
- blend_rows: bfloat16 [1024, 8, 8, 4096], P('dp', None, None, 'tensor'), may hold values from -6 to 6
- blend_gain: bfloat16 [4096], replicated, may hold values from 0.099609375 to 1.8984375
- blend_weight: bfloat16 [4096, 3, 2048], P('dp', None, 'tensor'), may hold values from -0.09375 to 0.09375
Outputs:
- rank_hidden: bfloat16 [256, 32, 5120], P(('dp', 'tensor'))
- cand_score: float32 [1024, 8], P('dp')
- blended_qkv: bfloat16 [1024, 24, 3, 2048], P('dp', None, None, 'tensor')
Inputs may be any that keep to these rules, and one draw needn't show every extreme that they name: `pair_index`: column 0 is a prompt of the pair's own group of 32 prompts (pair p belongs to group p // 8); columns 1 and 2 are two different candidates of that prompt. `cand_rank`: each row gives every rank once. `blend_owner`: each row names every group once.
All inputs are finite; a program needn't handle non-finite values.
Results may differ from a plain program's by a relative error of at most 0.024.
Values may be sent and summed in bfloat16 or wider, within the bound.
No kernel may reach another device: no remote copies, remote signals or barrier semaphores. Data moves between devices by JAX's collectives and lax.ppermute only.
A program may use at most 128 MiB of HBM per device.

v0:
```python
import math
import jax
import jax.numpy as jnp
from jax import lax
from jax.sharding import PartitionSpec as P

HR = 40
HDR = 128


def pair_attention(queries, keys_in, values_in, head_count):
    pair_count, length, row_width = queries.shape
    head_size = row_width // head_count
    query_heads = queries.reshape(pair_count, length, head_count, head_size)
    key_heads = keys_in.reshape(pair_count, length, head_count, head_size)
    value_heads = values_in.reshape(pair_count, length, head_count, head_size)
    scores = jnp.einsum(
        "pihd,pjhd->phij", query_heads, key_heads, preferred_element_type=jnp.float32
    ) * (1.0 / math.sqrt(HDR))
    highest = jnp.max(scores, axis=-1, keepdims=True)
    weights = jnp.exp(scores - highest)
    soft_weights = (weights / jnp.sum(weights, axis=-1, keepdims=True)).astype(jnp.bfloat16)
    context = jnp.einsum(
        "phij,pjhd->pihd", soft_weights, value_heads, preferred_element_type=jnp.float32
    )
    return context.astype(jnp.bfloat16).reshape(pair_count * length, row_width)


def encode(rows_in, blend_gain, blend_weight):
    whole_rows = lax.all_gather(rows_in, "tensor", axis=3, tiled=True)
    prompts, pick_count, length, features = whole_rows.shape
    flat_rows = whole_rows.reshape(prompts * pick_count * length, features)
    as_float = flat_rows.astype(jnp.float32)
    scale_rows = lax.rsqrt(jnp.mean(as_float * as_float, axis=-1, keepdims=True) + 1e-06)
    blend_normed = (as_float * scale_rows * blend_gain.astype(jnp.float32)).astype(jnp.bfloat16)
    columns = blend_weight.shape[1] * blend_weight.shape[2]
    portion = lax.all_gather(blend_weight, "dp", axis=0, tiled=True)
    projected = jnp.dot(
        blend_normed, portion.reshape(portion.shape[0], columns), preferred_element_type=jnp.float32
    )
    return projected.astype(jnp.bfloat16).reshape(
        prompts, pick_count * length, blend_weight.shape[1], blend_weight.shape[2]
    )


def body(
    rank_query,
    rank_key,
    rank_value,
    rank_resid,
    out_weight,
    rank_gain,
    score_weight,
    pair_index,
    cand_rank,
    cand_len,
    blend_owner,
    blend_rows,
    blend_gain,
    blend_weight,
):
    tensor_count = lax.axis_size("tensor")
    local_heads = HR // tensor_count
    length = rank_query.shape[1]
    context = pair_attention(rank_query, rank_key, rank_value, local_heads)
    own_pairs = rank_resid.shape[0]
    own_rows = own_pairs * length
    term_rows = jnp.dot(
        context,
        lax.all_gather(out_weight, "dp", axis=1, tiled=True),
        preferred_element_type=jnp.float32,
    )
    summed = lax.psum(term_rows.astype(jnp.bfloat16), "tensor").astype(jnp.float32)
    part_sum = lax.dynamic_slice_in_dim(summed, lax.axis_index("tensor") * own_rows, own_rows, 0)
    mixed_rows = rank_resid.reshape(own_rows, -1).astype(jnp.float32) + part_sum
    mean_square = jnp.mean(mixed_rows * mixed_rows, axis=-1, keepdims=True)
    normed = mixed_rows * lax.rsqrt(mean_square + 1e-05) * rank_gain.astype(jnp.float32)
    rank_hidden = normed.astype(jnp.bfloat16).reshape(rank_resid.shape)
    leading = normed.reshape(own_pairs, length, -1)[:, 0, :]
    pair_logit = jnp.sum(leading * score_weight.astype(jnp.float32), axis=-1)
    prompt_count = cand_rank.shape[0]
    cand_count = cand_rank.shape[1]
    slot_ids = jnp.arange(prompt_count * cand_count, dtype=jnp.int32)
    base_slot = pair_index[:, 0] * cand_count
    upward = jnp.where(
        (base_slot + pair_index[:, 1])[:, None] == slot_ids[None, :], pair_logit[:, None], 0.0
    )
    downward = jnp.where(
        (base_slot + pair_index[:, 2])[:, None] == slot_ids[None, :], pair_logit[:, None], 0.0
    )
    vote_sums = jnp.sum(upward - downward, axis=0).reshape(prompt_count, cand_count)
    cand_score = lax.psum(vote_sums, "tensor")
    places = jnp.arange(3, dtype=jnp.int32)
    matched = cand_rank[:, None, :] == places[None, :, None]
    labels = jnp.arange(cand_count, dtype=jnp.int32)
    chosen = jnp.sum(jnp.where(matched, labels[None, None, :], 0), axis=-1)
    chosen_len = jnp.sum(jnp.where(matched, cand_len[:, None, :], 0), axis=-1)
    prompt_ids = jnp.arange(prompt_count, dtype=jnp.int32)
    picked = blend_rows[prompt_ids[:, None], chosen]
    positions = jnp.arange(blend_rows.shape[2], dtype=jnp.int32)
    live_rows = positions[None, None, :] < chosen_len[:, :, None]
    picked = jnp.where(live_rows[..., None], picked, jnp.zeros((), jnp.bfloat16))
    owners = blend_owner[0]
    sender = jnp.sum(
        jnp.where(owners[None, :] == prompt_ids[:, None], prompt_ids[None, :], 0), axis=1
    )
    outgoing = picked[sender]
    arrived = lax.all_to_all(outgoing, "dp", split_axis=0, concat_axis=0, tiled=True)
    blended_qkv = encode(arrived, blend_gain, blend_weight)
    return (rank_hidden, cand_score, blended_qkv)


def solution(mesh):
    placed = (
        P("dp", None, "tensor"),
        P("dp", None, "tensor"),
        P("dp", None, "tensor"),
        P(("dp", "tensor"), None, None),
        P("tensor", "dp"),
        P(),
        P(),
        P(("dp", "tensor"), None),
        P("dp", None),
        P("dp", None),
        P("dp", None),
        P("dp", None, None, "tensor"),
        P(),
        P("dp", None, "tensor"),
    )
    return jax.shard_map(
        body,
        mesh=mesh,
        in_specs=placed,
        out_specs=(P(("dp", "tensor"), None, None), P("dp", None), P("dp", None, None, "tensor")),
        check_vma=False,
    )
```

profile of v0, /device:TPU:2, one launch (start us, length us, event | category | flops | bytes accessed | tf_op | source)
XLA Modules:
  0.0 343.9 jit_solution(1360914309973684097)
XLA Ops:
  7.2 0.0 copy-start
  7.2 0.0 copy-start.3
  7.2 0.0 copy-start.2
  7.2 0.0 all-gather.6.cloned.1.call-start
  7.2 0.9 select_reduce_fusion.2
  8.1 0.1 copy.60
  8.2 0.1 reshape.142
  8.3 0.1 copy.59
  8.4 0.1 iota_compare_fusion
  8.5 0.8 select_reduce_fusion
  9.3 0.6 pad_clamp_fusion
  9.9 2.0 gather_fusion
  11.9 1.3 broadcast_select_fusion
  13.3 0.0 copy-start.5
  13.3 0.0 copy-start.6
  13.3 1.7 gather_fusion.1
  15.0 21.0 %all_to_all.5 = bf16[32,3,8,512]{3,2,1,0:T(8,128)(2,1)} all-to-all(bf16[32,3,8,512]{3,2,1,0:T(8,128)(2,1)} %gather_fusion.1), channel_id=1, replica_groups=mesh['dp'=32,'tensor'=8] {'dp'}, dimensions={0} | all-to-all | bytes 1572864 | tf_op jit(solution)/shard_map/all_to_all | solution.py:108
  36.0 0.0 all-gather.6.cloned.1.call-update
  36.1 0.0 all-gather.4.cloned.1.call-start
  36.1 0.7 all-gather.4.cloned.1.call-update
  36.8 0.0 all-gather.8.cloned.1.call-start
  36.9 1.7 copy.63
  38.6 0.0 all-gather.8.cloned.1.call-update
  38.6 0.0 all-reduce.2.cloned.1.call-start
  38.7 1.0 fusion.32
  39.7 0.3 convolution_multiply_fusion
  40.0 1.3 fusion.6
  41.3 0.2 copy.58
  41.5 0.6 fusion.31
  44.0 0.7 convert_element_type.58
  44.7 66.2 %all-gather.6.cloned.1.call-done = bf16[32,3,8,4096]{3,2,1,0:T(8,128)(2,1)} async-done(((bf16[32,3,8,512]{3,2,1,0:T(8,128)(2,1)}), bf16[32,3,8,4096]{3,2,1,0:T(8,128)(2,1)}) %all-gather.6.cloned.1.call-update) | async-done | bytes 6291472 | tf_op jit(solution)/shard_map/all_gather | solution.py:30
  110.9 4.1 %fusion.1 = f32[32,3,8]{2,1,0:T(4,128)S(1)} fusion(bf16[32,3,8,4096]{3,2,1,0:T(8,128)(2,1)} %all-gather.6.cloned.1.call-done), kind=kLoop, calls=%fused_computation.5 | loop fusion | flops 9436416 | bytes 6294528 | tf_op jit(solution)/shard_map/reduce_sum | solution.py:34
  115.0 0.1 copy.61
  115.1 0.1 copy.62
  115.2 50.6 %all-gather.4.cloned.1.call-done = bf16[640,5120]{0,1:T(8,128)(2,1)} async-done(((bf16[640,160]{0,1:T(8,128)(2,1)}), bf16[640,5120]{0,1:T(8,128)(2,1)}) %all-gather.4.cloned.1.call-update) | async-done | bytes 6553616 | tf_op jit(solution)/shard_map/all_gather | solution.py:70
  165.7 6.6 %convolution_convert_fusion = bf16[256,5120]{1,0:T(8,128)(2,1)} fusion(bf16[640,5120]{0,1:T(8,128)(2,1)} %all-gather.4.cloned.1.call-done, bf16[32,8,5,128]{3,2,1,0:T(8,128)(2,1)S(1)} %bitcast.74), kind=kOutput, calls=%fused_computation.8 | convolution fusion | flops 1679032320 | bytes 9502720 | tf_op jit(solution)/shard_map/dot_general | solution.py:68
  172.3 0.0 all-reduce.2.cloned.1.call-update
  172.4 8.2 %fusion.3 = bf16[32,3,8,4096]{3,2,1,0:T(8,128)(2,1)} fusion(bf16[32,3,8,4096]{3,2,1,0:T(8,128)(2,1)} %all-gather.6.cloned.1.call-done, f32[4096]{0:T(1024)S(1)} %convert_element_type.58, f32[32,3,8]{2,1,0:T(4,128)S(1)} %copy.62), kind=kLoop, calls=%fused_computation.7 | loop fusion | flops 12582912 | bytes 12602368 | tf_op jit(solution)/shard_map/convert_element_type | solution.py:35
  180.5 47.1 %all-gather.8.cloned.1.call-done = bf16[4096,3,256]{0,2,1:T(8,128)(2,1)} async-done(((bf16[128,3,256]{0,2,1:T(8,128)(2,1)}), bf16[4096,3,256]{0,2,1:T(8,128)(2,1)}) %all-gather.8.cloned.1.call-update) | async-done | bytes 6291472 | tf_op jit(solution)/shard_map/all_gather | solution.py:37
  227.7 9.9 %convolution_convert_fusion.1 = bf16[768,768]{1,0:T(8,128)(2,1)} fusion(bf16[768,4096]{1,0:T(8,128)(2,1)} %bitcast.72, bf16[4096,768]{0,1:T(8,128)(2,1)} %bitcast.76), kind=kOutput, calls=%fused_computation.9 | convolution fusion | flops 4832428032 | bytes 13762560 | tf_op jit(solution)/shard_map/dot_general | solution.py:38
  237.6 3.7 %reshape.140 = bf16[32,24,3,256]{3,2,1,0:T(4,128)(2,1)} reshape(bf16[768,768]{1,0:T(8,128)(2,1)} %convolution_convert_fusion.1) | data formatting | bytes 2359296 | tf_op jit(solution)/shard_map/reshape | solution.py:41
  241.3 2.6 copy.64
  243.9 72.1 %all-reduce.2.cloned.1.call-done = bf16[256,5120]{1,0:T(8,128)(2,1)} async-done(((bf16[256,5120]{1,0:T(8,128)(2,1)}), bf16[256,5120]{1,0:T(8,128)(2,1)}) %all-reduce.2.cloned.1.call-update) | async-done | bytes 2621456 | tf_op jit(solution)/shard_map/psum | solution.py:73
  316.0 1.2 multiply_reduce_fusion
  317.2 1.8 fusion.7
  319.1 0.6 multiply_reduce_fusion.1
  319.7 0.6 select_subtract_fusion
  320.2 17.1 %psum.15 = f32[32,8]{0,1:T(8,128)} all-reduce(f32[32,8]{0,1:T(8,128)S(1)} %select_subtract_fusion), channel_id=1, replica_groups=mesh['dp'=32,'tensor'=8] {'tensor'}, use_global_device_ids=true, to_apply=%region_5.6 | all-reduce | flops 256 | bytes 2048 | tf_op jit(solution)/shard_map/psum | solution.py:92
  (15 shorter events, 0.1 us)
Async XLA Ops:
  7.2 2.7 copy-start
  7.2 31.5 %copy-start.3 = (bf16[8,32,640]{2,1,0:T(8,128)(2,1)S(1)}, bf16[8,32,640]{2,1,0:T(8,128)(2,1)}, u32[]{:S(2)}) copy-start(bf16[8,32,640]{2,1,0:T(8,128)(2,1)} %param.14) | copy-start | bytes 983044
  7.2 31.5 %copy-start.2 = (bf16[8,32,640]{2,1,0:T(8,128)(2,1)S(1)}, bf16[8,32,640]{2,1,0:T(8,128)(2,1)}, u32[]{:S(2)}) copy-start(bf16[8,32,640]{2,1,0:T(8,128)(2,1)} %param.15) | copy-start | bytes 983044
  7.2 103.7 %all-gather.6.cloned.1.call-start = ((), (), s32[]{:S(2)}) async-start(), calls=%async_computation.3 | async-start | bytes 7077888 | tf_op jit(solution)/shard_map/all_gather | solution.py:30
  13.3 28.3 %copy-start.5 = (bf16[5120]{0:T(1024)(128)(2,1)S(1)}, bf16[5120]{0:T(1024)(128)(2,1)}, u32[]{:S(2)}) copy-start(bf16[5120]{0:T(1024)(128)(2,1)} %param.19) | copy-start | bytes 30724
  13.3 28.3 %copy-start.6 = (s32[1,3]{1,0:T(1,128)S(1)}, s32[1,3]{1,0:T(1,128)}, u32[]{:S(2)}) copy-start(s32[1,3]{1,0:T(1,128)} %param.21) | copy-start | bytes 40
  36.1 129.7 %all-gather.4.cloned.1.call-start = ((), (), s32[]{:S(2)}) async-start(), calls=%async_computation.1 | async-start | bytes 6758400 | tf_op jit(solution)/shard_map/all_gather | solution.py:70
  36.8 190.9 %all-gather.8.cloned.1.call-start = ((), (), s32[]{:S(2)}) async-start(), calls=%async_computation.4 | async-start | bytes 6488064 | tf_op jit(solution)/shard_map/all_gather | solution.py:37
  38.6 277.4 %all-reduce.2.cloned.1.call-start = ((), (), s32[]{:S(2)}) async-start(), calls=%async_computation.2 | async-start | bytes 5242880 | tf_op jit(solution)/shard_map/psum | solution.py:73
  227.7 88.3 %copy-start.1 = (bf16[1,32,5120]{2,1,0:T(8,128)(2,1)S(1)}, bf16[1,32,5120]{2,1,0:T(8,128)(2,1)}, u32[]{:S(2)}) copy-start(bf16[1,32,5120]{2,1,0:T(8,128)(2,1)} %param.17) | copy-start | bytes 983044
  237.6 81.5 %copy-start.4 = (bf16[5120]{0:T(1024)(128)(2,1)S(1)}, bf16[5120]{0:T(1024)(128)(2,1)}, u32[]{:S(2)}) copy-start(bf16[5120]{0:T(1024)(128)(2,1)} %param.20) | copy-start | bytes 30724
Sparse Core Ops, SparseCore 0:
  36.2 74.6 all-gather.5
  113.4 52.2 all-gather.3
  168.8 58.8 all-gather.7
  229.9 86.0 all-reduce.1
where the time goes:
time: 345 us; the launch traced here: 344 us
  waiting for transfers between devices  237 us (69%)
  blocking collectives  38.1 us (11%)
  other arithmetic  20.9 us (6%)
  matrix products  19.1 us (6%)
  between operations  15.8 us (5%)
  local copies, waits for them, and re-layouts  13.1 us (4%)
    psum x1, waiting for transfers between devices, body(): lax.psum(term_rows.astype(jnp.bfloat16), 'tensor').astype(jnp.float32)  72.1 us
    all_gather x1, waiting for transfers between devices, encode(): whole_rows = lax.all_gather(rows_in, 'tensor', axis=3, tiled=True)  66.2 us
    all_gather x1, waiting for transfers between devices, body(): lax.all_gather(out_weight, 'dp', axis=1, tiled=True)  50.6 us
    all_gather x1, waiting for transfers between devices, encode(): portion = lax.all_gather(blend_weight, 'dp', axis=0, tiled=True)  47.1 us
    all_to_all x1, blocking collectives, body(): lax.all_to_all(outgoing, 'dp', split_axis=0, concat_axis=0, tiled=True)  21 us
    psum x1, blocking collectives, body(): cand_score = lax.psum(vote_sums, 'tensor')  17.1 us
    dot_general x1, matrix products, encode(): jnp.dot(blend_normed, portion.reshape(portion.shape[0], columns), preferr...  9.89 us
    convert_element_type x1, other arithmetic, encode(): (as_float * scale_rows * blend_gain.astype(jnp.float32)).astype(jnp.bfloa...  8.16 us
  transfers between devices with their start and end apart: 4, of which 4 were waited for; matrix products, arithmetic and copies ran while one was open for 12% of the time, Pallas kernels for 0%

commit v1 on v0

--- a/solution.py
+++ b/solution.py
@@ -6,6 +6,14 @@
 
 HR = 40
 HDR = 128
+
+
+def gather_by_exchange(shard, axis, dim):
+    length = lax.axis_size(axis)
+    repeats = [length if d == dim else 1 for d in range(shard.ndim)]
+    return lax.all_to_all(
+        jnp.tile(shard, repeats), axis, split_axis=dim, concat_axis=dim, tiled=True
+    )
 
 
 def pair_attention(queries, keys_in, values_in, head_count):
@@ -66,9 +74,7 @@
     own_pairs = rank_resid.shape[0]
     own_rows = own_pairs * length
     term_rows = jnp.dot(
-        context,
-        lax.all_gather(out_weight, "dp", axis=1, tiled=True),
-        preferred_element_type=jnp.float32,
+        context, gather_by_exchange(out_weight, "dp", 1), preferred_element_type=jnp.float32
     )
     summed = lax.psum(term_rows.astype(jnp.bfloat16), "tensor").astype(jnp.float32)
     part_sum = lax.dynamic_slice_in_dim(summed, lax.axis_index("tensor") * own_rows, own_rows, 0)

time: 345 us -> 349 us (1.012)
  starting transfers between devices: 0.16 us -> 7.92 us
    all_to_all x0 -> x1, waiting for transfers between devices: none -> 75.9 us  [gather_by_exchange(): lax.all_to_all(jnp.tile(shard, repeats), axis, split_axis=dim, concat_axi...]
    all_gather x1 -> x0, waiting for transfers between devices: 50.6 us -> none  [body(): lax.all_gather(out_weight, 'dp', axis=1, tiled=True)]
    psum x1, waiting for transfers between devices: 72.1 us -> 59.1 us  [body(): lax.psum(term_rows.astype(jnp.bfloat16), 'tensor').astype(jnp.float32)]
    all_gather x1, waiting for transfers between devices: 66.2 us -> 53.2 us  [encode(): whole_rows = lax.all_gather(rows_in, 'tensor', axis=3, tiled=True)]
    all_to_all x0 -> x1, starting transfers between devices: none -> 7.8 us  [gather_by_exchange(): lax.all_to_all(jnp.tile(shard, repeats), axis, split_axis=dim, concat_axi...]
    another operation x0 -> x1, local copies, waits for them, and re-layouts: none -> 4.28 us  [gather_by_exchange(): jnp.tile(shard, repeats)]
  transfers between devices with their start and end apart: 4 -> 4, of which waited for: 4 -> 4; matrix products, arithmetic and copies ran while one was open for 12% -> 7% of each run, Pallas kernels for 0% -> 0%
where the time goes in v1:
time: 349 us; the launch traced here: 347 us
  waiting for transfers between devices  237 us (68%)
  blocking collectives  37.8 us (11%)
  other arithmetic  17.9 us (5%)
  matrix products  17.6 us (5%)
  between operations  15.9 us (5%)
  local copies, waits for them, and re-layouts  13.7 us (4%)
  starting transfers between devices  7.92 us (2%)
    all_to_all x1, waiting for transfers between devices, gather_by_exchange(): lax.all_to_all(jnp.tile(shard, repeats), axis, split_axis=dim, concat_axi...  75.9 us
    psum x1, waiting for transfers between devices, body(): lax.psum(term_rows.astype(jnp.bfloat16), 'tensor').astype(jnp.float32)  59.1 us
    all_gather x1, waiting for transfers between devices, encode(): whole_rows = lax.all_gather(rows_in, 'tensor', axis=3, tiled=True)  53.2 us
    all_gather x1, waiting for transfers between devices, encode(): portion = lax.all_gather(blend_weight, 'dp', axis=0, tiled=True)  48.3 us
    all_to_all x1, blocking collectives, body(): lax.all_to_all(outgoing, 'dp', split_axis=0, concat_axis=0, tiled=True)  20.5 us
    psum x1, blocking collectives, body(): cand_score = lax.psum(vote_sums, 'tensor')  17.4 us
    dot_general x1, matrix products, encode(): jnp.dot(blend_normed, portion.reshape(portion.shape[0], columns), preferr...  9.04 us
    convert_element_type x1, other arithmetic, encode(): (as_float * scale_rows * blend_gain.astype(jnp.float32)).astype(jnp.bfloa...  8.13 us
  transfers between devices with their start and end apart: 4, of which 4 were waited for; matrix products, arithmetic and copies ran while one was open for 7% of the time, Pallas kernels for 0%

profile of v1, /device:TPU:2, one launch (start us, length us, event | category | flops | bytes accessed | tf_op | source)
XLA Modules:
  0.0 347.4 jit_solution(12593809048193711153)
XLA Ops:
  7.2 0.0 copy-start
  7.2 4.3 %tile.2 = bf16[640,32,160]{0,2,1:T(8,128)(2,1)} broadcast(bf16[640,160]{0,1:T(8,128)(2,1)} %param.18), dimensions={0,2} | broadcast | bytes 6758400 | tf_op jit(solution)/shard_map/tile | solution.py:15
  11.5 7.8 %all-to-all-start = ((bf16[640,32,160]{0,2,1:T(8,128)(2,1)}), bf16[640,32,160]{0,2,1:T(8,128)(2,1)}, u32[]{:S(2)}, u32[]{:S(2)}) async-start(bf16[640,32,160]{0,2,1:T(8,128)(2,1)} %tile.2), calls=%async_computation | async-start | bytes 13107200 | tf_op jit(solution)/shard_map/all_to_all | solution.py:14
  19.3 0.0 all-reduce.2.cloned.1.call-start
  19.3 0.0 copy-done.2
  19.3 0.0 copy-done.3
  19.3 0.4 fusion.32
  19.7 0.3 convolution_multiply_fusion
  20.0 1.3 fusion.6
  21.3 0.2 copy.59
  21.5 0.0 copy-start.9
  21.5 0.0 copy-start.10
  21.5 75.9 %all-to-all-done = bf16[640,32,160]{0,2,1:T(8,128)(2,1)} async-done(((bf16[640,32,160]{0,2,1:T(8,128)(2,1)}), bf16[640,32,160]{0,2,1:T(8,128)(2,1)}, u32[]{:S(2)}, u32[]{:S(2)}) %all-to-all-start) | async-done | bytes 6553632 | tf_op jit(solution)/shard_map/all_to_all | solution.py:14
  97.5 6.6 %convolution_convert_fusion = bf16[256,5120]{1,0:T(8,128)(2,1)} fusion(bf16[640,5120]{0,1:T(8,128)(2,1)} %bitcast.2, bf16[32,8,5,128]{3,2,1,0:T(8,128)(2,1)S(1)} %bitcast.75), kind=kOutput, calls=%fused_computation.8 | convolution fusion | flops 1679032320 | bytes 9502720 | tf_op jit(solution)/shard_map/dot_general | solution.py:76
  104.1 0.0 copy-start.1
  104.1 0.0 copy-start.5
  104.1 0.0 all-reduce.2.cloned.1.call-update
  104.1 0.0 all-gather.3.cloned.1.call-start
  104.2 0.1 copy.61
  104.3 0.1 reshape.149
  104.4 0.1 copy.60
  104.5 1.0 gather_fusion
  105.6 0.0 copy-done.11
  105.6 0.1 select_reduce_fusion
  105.7 0.1 iota_compare_fusion
  105.8 1.1 broadcast_select_fusion
  106.9 1.7 gather_fusion.1
  108.6 20.5 %all_to_all.14 = bf16[32,3,8,512]{3,2,1,0:T(8,128)(2,1)} all-to-all(bf16[32,3,8,512]{3,2,1,0:T(8,128)(2,1)S(1)} %gather_fusion.1), channel_id=1, replica_groups=mesh['dp'=32,'tensor'=8] {'dp'}, dimensions={0} | all-to-all | bytes 1572864 | tf_op jit(solution)/shard_map/all_to_all | solution.py:114
  129.1 0.0 all-gather.3.cloned.1.call-update
  129.1 0.0 all-gather.5.cloned.1.call-start
  129.1 0.8 copy.64
  130.0 0.0 all-gather.5.cloned.1.call-update
  130.0 0.6 fusion.31
  132.5 59.1 %all-reduce.2.cloned.1.call-done = bf16[256,5120]{1,0:T(8,128)(2,1)} async-done(((bf16[256,5120]{1,0:T(8,128)(2,1)}), bf16[256,5120]{1,0:T(8,128)(2,1)}) %all-reduce.2.cloned.1.call-update) | async-done | bytes 2621456 | tf_op jit(solution)/shard_map/psum | solution.py:79
  191.6 1.2 multiply_reduce_fusion
  192.8 1.9 fusion.7
  194.7 0.6 multiply_reduce_fusion.1
  195.3 0.6 select_subtract_fusion
  195.9 17.4 %psum.15 = f32[32,8]{0,1:T(8,128)} all-reduce(f32[32,8]{0,1:T(8,128)S(1)} %select_subtract_fusion), channel_id=1, replica_groups=mesh['dp'=32,'tensor'=8] {'tensor'}, use_global_device_ids=true, to_apply=%region_5.6 | all-reduce | flops 256 | bytes 2048 | tf_op jit(solution)/shard_map/psum | solution.py:98
  213.3 53.2 %all-gather.3.cloned.1.call-done = bf16[32,3,8,4096]{3,2,1,0:T(8,128)(2,1)} async-done(((bf16[32,3,8,512]{3,2,1,0:T(8,128)(2,1)}), bf16[32,3,8,4096]{3,2,1,0:T(8,128)(2,1)}) %all-gather.3.cloned.1.call-update) | async-done | bytes 6291472 | tf_op jit(solution)/shard_map/all_gather | solution.py:38
  266.5 4.1 %fusion.1 = f32[32,3,8]{2,1,0:T(4,128)S(1)} fusion(bf16[32,3,8,4096]{3,2,1,0:T(8,128)(2,1)} %all-gather.3.cloned.1.call-done), kind=kLoop, calls=%fused_computation.5 | loop fusion | flops 9436416 | bytes 6294528 | tf_op jit(solution)/shard_map/reduce_sum | solution.py:42
  270.6 0.1 copy.62
  270.7 0.1 copy.63
  270.8 8.1 %fusion.3 = bf16[32,3,8,4096]{3,2,1,0:T(8,128)(2,1)} fusion(bf16[32,3,8,4096]{3,2,1,0:T(8,128)(2,1)} %all-gather.3.cloned.1.call-done, f32[4096]{0:T(1024)S(1)} %convert_element_type.58, f32[32,3,8]{2,1,0:T(4,128)S(1)} %copy.63), kind=kLoop, calls=%fused_computation.7 | loop fusion | flops 12582912 | bytes 12602368 | tf_op jit(solution)/shard_map/convert_element_type | solution.py:43
  279.0 48.3 %all-gather.5.cloned.1.call-done = bf16[4096,3,256]{0,2,1:T(8,128)(2,1)} async-done(((bf16[128,3,256]{0,2,1:T(8,128)(2,1)}), bf16[4096,3,256]{0,2,1:T(8,128)(2,1)}) %all-gather.5.cloned.1.call-update) | async-done | bytes 6291472 | tf_op jit(solution)/shard_map/all_gather | solution.py:45
  327.2 9.0 %convolution_convert_fusion.1 = bf16[768,768]{1,0:T(8,128)(2,1)S(1)} fusion(bf16[768,4096]{1,0:T(8,128)(2,1)} %bitcast.73, bf16[4096,768]{0,1:T(8,128)(2,1)} %bitcast.77), kind=kOutput, calls=%fused_computation.9 | convolution fusion | flops 4832428032 | bytes 13762560 | tf_op jit(solution)/shard_map/dot_general | solution.py:46
  336.3 1.9 reshape.147
  338.2 2.6 copy.65
  (25 shorter events, 0.1 us)
Async XLA Ops:
  7.2 97.4 %copy-start = (bf16[32,8,8,512]{3,2,1,0:T(8,128)(2,1)S(1)}, bf16[32,8,8,512]{3,2,1,0:T(8,128)(2,1)}, u32[]{:S(2)}) copy-start(bf16[32,8,8,512]{3,2,1,0:T(8,128)(2,1)} %param.25) | copy-start | bytes 6291460
  11.5 7.9 %copy-start.2 = (bf16[8,32,640]{2,1,0:T(8,128)(2,1)S(1)}, bf16[8,32,640]{2,1,0:T(8,128)(2,1)}, u32[]{:S(2)}) copy-start(bf16[8,32,640]{2,1,0:T(8,128)(2,1)} %param.15) | copy-start | bytes 983044
  11.5 7.9 %copy-start.3 = (bf16[8,32,640]{2,1,0:T(8,128)(2,1)S(1)}, bf16[8,32,640]{2,1,0:T(8,128)(2,1)}, u32[]{:S(2)}) copy-start(bf16[8,32,640]{2,1,0:T(8,128)(2,1)} %param.14) | copy-start | bytes 983044
  11.5 86.0 %all-to-all-start = ((bf16[640,32,160]{0,2,1:T(8,128)(2,1)}), bf16[640,32,160]{0,2,1:T(8,128)(2,1)}, u32[]{:S(2)}, u32[]{:S(2)}) async-start(bf16[640,32,160]{0,2,1:T(8,128)(2,1)} %tile.2), calls=%async_computation | async-start | bytes 13107200 | tf_op jit(solution)/shard_map/all_to_all | solution.py:14
  19.3 172.3 %all-reduce.2.cloned.1.call-start = ((), (), s32[]{:S(2)}) async-start(), calls=%async_computation.2 | async-start | bytes 5242880 | tf_op jit(solution)/shard_map/psum | solution.py:79
  21.5 82.7 %copy-start.9 = (s32[32,8]{0,1:T(8,128)S(1)}, s32[32,8]{0,1:T(8,128)}, u32[]{:S(2)}) copy-start(s32[32,8]{0,1:T(8,128)} %param.23) | copy-start | bytes 3076
  21.5 82.7 %copy-start.10 = (s32[32,8]{0,1:T(8,128)S(1)}, s32[32,8]{0,1:T(8,128)}, u32[]{:S(2)}) copy-start(s32[32,8]{0,1:T(8,128)} %param.22) | copy-start | bytes 3076
  97.5 8.1 %copy-start.11 = (s32[1,32]{1,0:T(1,128)S(1)}, s32[1,32]{1,0:T(1,128)}, u32[]{:S(2)}) copy-start(s32[1,32]{1,0:T(1,128)} %param.24) | copy-start | bytes 388
  104.1 25.1 %copy-start.4 = (bf16[128,3,256]{2,0,1:T(8,128)(2,1)S(1)}, bf16[128,3,256]{2,0,1:T(8,128)(2,1)}, u32[]{:S(2)}) copy-start(bf16[128,3,256]{2,0,1:T(8,128)(2,1)} %param.27) | copy-start | bytes 589828
  104.1 25.9 %copy-start.6 = (bf16[5120]{0:T(1024)(128)(2,1)S(1)}, bf16[5120]{0:T(1024)(128)(2,1)}, u32[]{:S(2)}) copy-start(bf16[5120]{0:T(1024)(128)(2,1)} %param.19) | copy-start | bytes 30724
  104.1 25.9 %copy-start.8 = (s32[1,3]{1,0:T(1,128)S(1)}, s32[1,3]{1,0:T(1,128)}, u32[]{:S(2)}) copy-start(s32[1,3]{1,0:T(1,128)} %param.21) | copy-start | bytes 40
  104.1 28.4 %copy-start.7 = (bf16[4096]{0:T(1024)(128)(2,1)S(1)}, bf16[4096]{0:T(1024)(128)(2,1)}, u32[]{:S(2)}) copy-start(bf16[4096]{0:T(1024)(128)(2,1)} %param.26) | copy-start | bytes 24580
  104.1 87.5 %copy-start.1 = (bf16[1,32,5120]{2,1,0:T(8,128)(2,1)S(1)}, bf16[1,32,5120]{2,1,0:T(8,128)(2,1)}, u32[]{:S(2)}) copy-start(bf16[1,32,5120]{2,1,0:T(8,128)(2,1)} %param.17) | copy-start | bytes 983044
  104.1 90.6 %copy-start.5 = (bf16[5120]{0:T(1024)(128)(2,1)S(1)}, bf16[5120]{0:T(1024)(128)(2,1)}, u32[]{:S(2)}) copy-start(bf16[5120]{0:T(1024)(128)(2,1)} %param.20) | copy-start | bytes 30724
  104.1 162.4 %all-gather.3.cloned.1.call-start = ((), (), s32[]{:S(2)}) async-start(), calls=%async_computation.3 | async-start | bytes 7077888 | tf_op jit(solution)/shard_map/all_gather | solution.py:38
  129.1 198.2 %all-gather.5.cloned.1.call-start = ((), (), s32[]{:S(2)}) async-start(), calls=%async_computation.4 | async-start | bytes 6488064 | tf_op jit(solution)/shard_map/all_gather | solution.py:45
Sparse Core Ops, SparseCore 0:
  104.3 87.2 all-reduce.1
  193.4 73.1 all-gather.2
  269.6 57.6 all-gather.4
